TPU v7x, 256 devices: a whole 4x4x8 slice. The times are simulated.
256 devices in a mesh: dp: 16 (over y, z_hi, core), tensor: 16 (over z_lo, x).
Axes of the slice: x: 4, y: 4, z: 8 (z_hi: 2, z_lo: 4; z = z_hi * 4 + z_lo), core: 2. Of those that a mesh axis runs over, the one named last changes fastest.
Arguments:
- tokens: bfloat16 [1024, 8192], P('tensor', 'dp'), may hold values from -6 to 6
- gate_weight: bfloat16 [8192, 29568], P('dp', 'tensor'), may hold values from -0.0625 to 0.0625
- up_weight: bfloat16 [8192, 29568], P('dp', 'tensor'), may hold values from -0.0625 to 0.0625
- down_weight: bfloat16 [29568, 8192], P('tensor', 'dp'), may hold values from -0.03125 to 0.03125
- labels: int32 [1024], P('tensor'), may hold values from 0 to 255
Outputs:
- erased: bfloat16 [1024, 8192], P('tensor', 'dp')
All inputs are finite; a program needn't handle non-finite values.
Results may differ from a plain program's by a relative error of at most 0.029.
Values may be sent and summed in bfloat16 or wider, within the bound.
A program may use at most 64 MiB of HBM per device.

v0:
```python
import jax
import jax.numpy as jnp
from jax import lax
from jax.sharding import PartitionSpec as P

NCLS = 256
epsilon = 1e-05
ridge_share = 0.5


def shards(tokens, gate_weight, up_weight, down_weight, labels):
    groups = lax.axis_size("tensor")
    shard_rows = tokens.shape[0]
    row_total = shard_rows * groups
    hidden_cols = gate_weight.shape[1]
    high = lax.Precision.HIGHEST
    gathered = lax.all_gather(tokens, "tensor", axis=0, tiled=True)
    joined = jnp.concatenate([gate_weight, up_weight], axis=1)
    partial_value = jnp.dot(gathered, joined, preferred_element_type=jnp.float32).astype(
        jnp.bfloat16
    )
    summed = lax.psum_scatter(
        lax.optimization_barrier(partial_value).astype(jnp.float32).astype(jnp.bfloat16),
        "dp",
        scatter_dimension=0,
        tiled=True,
    ).astype(jnp.float32)
    hidden = (jax.nn.silu(summed[:, :hidden_cols]) * summed[:, hidden_cols:]).astype(jnp.bfloat16)
    partial_out = jnp.dot(
        lax.all_gather(hidden, "dp", axis=0, tiled=True),
        down_weight,
        preferred_element_type=jnp.float32,
    )
    output = lax.psum_scatter(partial_out, "tensor", scatter_dimension=0, tiled=True)
    classes = jnp.arange(NCLS, dtype=jnp.int32)
    onehot = (labels[:, None] == classes[None, :]).astype(jnp.float32)
    col_total, counts = lax.psum((jnp.sum(output, axis=0), jnp.sum(onehot, axis=0)), "tensor")
    mean_out = col_total / row_total
    shares = counts / row_total
    centred = output - mean_out
    cross_part = jnp.dot(centred.T, onehot - shares, precision=high)
    cross_sum, square_sum = lax.psum((cross_part, jnp.sum(centred * centred, axis=0)), "tensor")
    cross = cross_sum / row_total
    variance = square_sum / row_total
    spread = jnp.sqrt(variance + epsilon)
    whitened = cross / spread[:, None]
    white_rows = centred / spread
    gram_mat, coords = lax.psum(
        (
            jnp.dot(whitened.T, whitened, precision=high),
            jnp.dot(white_rows, whitened, precision=high),
        ),
        "dp",
    )
    ridge_term = ridge_share * jnp.trace(gram_mat) / NCLS
    factor = jnp.linalg.cholesky(gram_mat + ridge_term * jnp.eye(NCLS, dtype=jnp.float32))
    solved = jax.scipy.linalg.cho_solve((factor, True), coords.T)
    correction = jnp.dot(whitened, solved, precision=high).T * spread
    return (output - correction).astype(jnp.bfloat16)


def solution(mesh):
    return jax.shard_map(
        shards,
        mesh=mesh,
        in_specs=(
            P("tensor", "dp"),
            P("dp", "tensor"),
            P("dp", "tensor"),
            P("tensor", "dp"),
            P("tensor"),
        ),
        out_specs=P("tensor", "dp"),
        check_vma=False,
    )
```

profile of v0, /device:TPU:1, one launch (start us, length us, event | category | flops | bytes accessed | tf_op | source)
XLA Modules:
  0.0 900.5 jit_solution(123671681127873409)
XLA Ops:
  6.5 0.7 all-gather.3.cloned.1.call-update
  7.3 76.4 %all-gather.3.cloned.1.call-done = bf16[1024,512]{1,0:T(8,128)(2,1)} async-done(((bf16[64,512]{1,0:T(8,128)(2,1)}), bf16[1024,512]{1,0:T(8,128)(2,1)}) %all-gather.3.cloned.1.call-update) | async-done | bytes 1048592 | tf_op jit(solution)/shard_map/all_gather | solution.py:17
  83.7 9.6 %convert_bitcast_fusion = bf16[1024,3696]{0,1:T(8,128)(2,1)} fusion(bf16[1024,512]{1,0:T(8,128)(2,1)} %all-gather.3.cloned.1.call-done, bf16[512,1848]{0,1:T(8,128)(2,1)} %param.7, bf16[512,1848]{0,1:T(8,128)(2,1)} %param.6), kind=kOutput, calls=%fused_computation.2 | convolution fusion | flops 3886891008 | bytes 12402688 | tf_op jit(solution)/shard_map/dot_general | solution.py:19
  93.3 10.3 %copy.34 = bf16[1024,3696]{1,0:T(8,128)(2,1)} copy(bf16[1024,3696]{0,1:T(8,128)(2,1)} %convert_bitcast_fusion) | data formatting | bytes 15138816
  103.6 138.4 %reduce-scatter.7.cloned.1.call-done = bf16[64,3696]{1,0:T(8,128)(2,1)} async-done(((bf16[1024,3696]{1,0:T(8,128)(2,1)}), bf16[64,3696]{1,0:T(8,128)(2,1)}) %reduce-scatter.7.cloned.1.call-update) | async-done | bytes 473104 | tf_op jit(solution)/shard_map/reduce_scatter | solution.py:22
  242.1 1.1 convert_element_type.23
  243.2 0.9 fusion.5
  244.2 73.9 %all-gather.5.cloned.1.call-done = bf16[1024,1848]{1,0:T(8,128)(2,1)} async-done(((bf16[64,1848]{1,0:T(8,128)(2,1)}), bf16[1024,1848]{1,0:T(8,128)(2,1)}) %all-gather.5.cloned.1.call-update) | async-done | bytes 3784720 | tf_op jit(solution)/shard_map/all_gather | solution.py:30
  318.0 5.8 fusion.34
  324.0 73.1 %reduce-scatter.5.cloned.1.call-done = f32[64,512]{1,0:T(8,128)} async-done(((f32[1024,512]{1,0:T(8,128)}), f32[64,512]{1,0:T(8,128)}) %reduce-scatter.5.cloned.1.call-update) | async-done | bytes 131088 | tf_op jit(solution)/shard_map/reduce_scatter | solution.py:34
  397.0 0.9 reduce_sum.37
  398.0 31.4 %psum.42 = f32[512]{0:T(512)S(1)} all-reduce(f32[512]{0:T(512)S(1)} %reduce_sum.37), channel_id=1, replica_groups=mesh['dp'=16,'tensor'=16] {'tensor'}, use_global_device_ids=true, to_apply=%region_3.4 | all-reduce | flops 512 | bytes 4096 | tf_op jit(solution)/shard_map/psum | solution.py:37
  429.3 0.9 multiply_reduce_fusion
  430.3 32.0 %all-reduce.1 = (f32[256]{0:T(256)S(1)}, f32[512]{0:T(512)S(1)}) all-reduce(f32[256]{0:T(256)S(1)} %convert_reduce_fusion, f32[512]{0:T(512)S(1)} %multiply_reduce_fusion), channel_id=1, replica_groups=mesh['dp'=16,'tensor'=16] {'tensor'}, use_global_device_ids=true, to_apply=%region_5.6 | all-reduce | flops 768 | bytes 6144 | tf_op jit(solution)/shard_map/psum | solution.py:37
  462.3 2.4 fusion.10
  464.9 173.9 %all-reduce.6.cloned.1.call-done = f32[512,256]{1,0:T(8,128)} async-done(((f32[512,256]{1,0:T(8,128)}), f32[512,256]{1,0:T(8,128)}) %all-reduce.6.cloned.1.call-update) | async-done | bytes 524304 | tf_op jit(solution)/shard_map/psum | solution.py:42
  638.8 2.2 fusion.7
  641.1 3.1 fusion.32
  644.2 182.0 %all-reduce.8.cloned.1.call-done = (f32[256,256]{0,1:T(8,128)}, f32[256,64]{0,1:T(8,128)}) async-done(((f32[256,256]{0,1:T(8,128)}, f32[256,64]{0,1:T(8,128)}), (f32[256,256]{0,1:T(8,128)}, f32[256,64]{0,1:T(8,128)})) %all-reduce.8.cloned.1.call-update) | async-done | bytes 327696 | tf_op jit(solution)/shard_map/psum | solution.py:48
  826.2 1.6 select_reduce_fusion
  828.5 1.0 select_add_fusion
  829.6 1.0 fusion.6
  830.6 11.7 %cholesky.49 = f32[128,128]{1,0:T(8,128)S(1)} custom-call(f32[128,128]{1,0:T(8,128)S(1)} %cholesky.115), custom_call_target="Cholesky" | custom-call | tf_op jit(solution)/shard_map/jit(cholesky)/cholesky | solution.py:56
  842.4 9.8 %custom-call.18 = f32[1,128,128]{1,2,0:T(8,128)S(1)} custom-call(f32[1,128,128]{2,1,0:T(8,128)S(1)} %get-tuple-element.44), custom_call_target="InvertDiagBlocksLowerTriangular" | custom-call | tf_op jit(solution)/shard_map/jit(cholesky)/cholesky | solution.py:56
  852.6 11.7 %cholesky.103 = f32[128,128]{1,0:T(8,128)S(1)} custom-call(f32[128,128]{1,0:T(8,128)S(1)} %convolution_subtract_fusion), custom_call_target="Cholesky" | custom-call | tf_op jit(solution)/shard_map/jit(cholesky)/cholesky | solution.py:56
  864.7 0.7 compare_reduce_fusion
  866.9 4.3 while.1
  866.9 0.6 fusion.46
  867.5 1.4 dynamic-slice.7
  869.7 1.4 dynamic-slice.7
  871.3 19.7 %custom-call.19 = f32[2,128,128]{1,2,0:T(8,128)S(1)} custom-call(f32[2,128,128]{2,1,0:T(8,128)S(1)} %get-tuple-element.12), custom_call_target="InvertDiagBlocksLowerTriangular" | custom-call | tf_op jit(solution)/shard_map/jit(_cho_solve)/triangular_solve | solution.py:57
  892.3 1.3 fusion.4
  (54 shorter events, 3.8 us)
Async XLA Ops:
  6.5 311.5 %copy-start = (bf16[1848,512]{1,0:T(8,128)(2,1)S(1)}, bf16[1848,512]{1,0:T(8,128)(2,1)}, u32[]{:S(2)}) copy-start(bf16[1848,512]{1,0:T(8,128)(2,1)} %param.8) | copy-start | bytes 5677060
  6.5 77.2 %all-gather.3.cloned.1.call-start = ((), (), s32[]{:S(2)}) async-start(), calls=%async_computation.2 | async-start | bytes 1114112 | tf_op jit(solution)/shard_map/all_gather | solution.py:17
  7.3 234.8 %reduce-scatter.7.cloned.1.call-start = ((), (), s32[]{:S(2)}) async-start(), calls=%async_computation.6 | async-start | bytes 8077312 | tf_op jit(solution)/shard_map/reduce_scatter | solution.py:22
  103.6 214.4 %all-gather.5.cloned.1.call-start = ((), (), s32[]{:S(2)}) async-start(), calls=%async_computation.3 | async-start | bytes 4177920 | tf_op jit(solution)/shard_map/all_gather | solution.py:30
  244.1 79.8 %copy-start.3 = (s32[64]{0:T(128)S(1)}, s32[64]{0:T(128)}, u32[]{:S(2)}) copy-start(s32[64]{0:T(128)} %param.9) | copy-start | bytes 772
  244.1 152.9 %reduce-scatter.5.cloned.1.call-start = ((), (), s32[]{:S(2)}) async-start(), calls=%async_computation.4 | async-start | bytes 2228224 | tf_op jit(solution)/shard_map/reduce_scatter | solution.py:34
  323.8 315.0 %all-reduce.6.cloned.1.call-start = ((), (), s32[]{:S(2)}) async-start(), calls=%async_computation.5 | async-start | bytes 1048576 | tf_op jit(solution)/shard_map/psum | solution.py:42
  464.7 361.5 %all-reduce.8.cloned.1.call-start = ((), (), s32[]{:S(2)}) async-start(), calls=%async_computation.7 | async-start | bytes 655360 | tf_op jit(solution)/shard_map/psum | solution.py:48
  644.2 248.1 %copy-start.1 = (f32[64,512]{1,0:T(8,128)S(1)}, f32[64,512]{1,0:T(8,128)}, u32[]{:S(2)}) copy-start(f32[64,512]{1,0:T(8,128)} %reduce-scatter.5.cloned.1.call-done) | copy-start | bytes 393220
  644.2 248.1 %copy-start.4 = (f32[512,256]{1,0:T(8,128)S(1)}, f32[512,256]{1,0:T(8,128)}, u32[]{:S(2)}) copy-start(f32[512,256]{1,0:T(8,128)} %all-reduce.6.cloned.1.call-done) | copy-start | bytes 1572868
  826.2 64.8 %copy-start.2 = (f32[256,64]{0,1:T(8,128)S(1)}, f32[256,64]{0,1:T(8,128)}, u32[]{:S(2)}) copy-start(f32[256,64]{0,1:T(8,128)} %get-tuple-element.40) | copy-start | bytes 196612
Sparse Core Ops, SparseCore 0:
  9.1 74.5 all-gather.2
  103.7 138.3 reduce-scatter.6
  245.1 72.8 all-gather.4
  323.9 73.0 reduce-scatter.4
  464.8 173.9 all-reduce.5
  644.3 181.8 all-reduce.7
where the time goes:
time: 901 us; the launch traced here: 900 us
  waiting for transfers between devices  718 us (80%)
  blocking collectives  63.4 us (7%)
  other arithmetic  61.3 us (7%)
  matrix products  26.1 us (3%)
  between operations  15.7 us (2%)
  local copies, waits for them, and re-layouts  15.1 us (2%)
    psum x1, waiting for transfers between devices, shards(): lax.psum((jnp.dot(whitened.T, whitened, precision=high), jnp.dot(white_ro...  182 us
    psum x1, waiting for transfers between devices, shards(): lax.psum((cross_part, jnp.sum(centred * centred, axis=0)), 'tensor')  174 us
    reduce_scatter x1, waiting for transfers between devices, shards(): lax.psum_scatter(lax.optimization_barrier(partial_value).astype(jnp.float...  138 us
    all_gather x1, waiting for transfers between devices, shards(): gathered = lax.all_gather(tokens, 'tensor', axis=0, tiled=True)  76.4 us
    all_gather x1, waiting for transfers between devices, shards(): lax.all_gather(hidden, 'dp', axis=0, tiled=True)  73.9 us
    reduce_scatter x1, waiting for transfers between devices, shards(): lax.psum_scatter(partial_out, 'tensor', scatter_dimension=0, tiled=True)  73.1 us
    psum x2, blocking collectives, shards(): lax.psum((jnp.sum(output, axis=0), jnp.sum(onehot, axis=0)), 'tensor')  63.4 us
    another operation x6, other arithmetic, shards(): jnp.linalg.cholesky(gram_mat + ridge_term * jnp.eye(NCLS, dtype=jnp.float...  34 us
  transfers between devices with their start and end apart: 6, of which 6 were waited for; matrix products, arithmetic and copies ran while one was open for 0% of the time, Pallas kernels for 0%

commit v1 on v0

--- a/solution.py
+++ b/solution.py
@@ -14,7 +14,9 @@
     row_total = shard_rows * groups
     hidden_cols = gate_weight.shape[1]
     high = lax.Precision.HIGHEST
-    gathered = lax.all_gather(tokens, "tensor", axis=0, tiled=True)
+    gathered = jnp.concatenate(
+        lax.all_to_all(jnp.stack([tokens] * lax.axis_size("tensor")), "tensor", 0, 0), axis=0
+    )
     joined = jnp.concatenate([gate_weight, up_weight], axis=1)
     partial_value = jnp.dot(gathered, joined, preferred_element_type=jnp.float32).astype(
         jnp.bfloat16

time: 901 us -> 850 us (0.943)
  waiting for transfers between devices: 718 us -> 634 us
  blocking collectives: 63.4 us -> 97 us
    all_gather x1 -> x0, waiting for transfers between devices: 76.4 us -> none  [shards(): gathered = lax.all_gather(tokens, 'tensor', axis=0, tiled=True)]
    all_to_all x0 -> x1, blocking collectives: none -> 33.7 us  [shards(): lax.all_to_all(jnp.stack([tokens] * lax.axis_size('tensor')), 'tensor', 0...]
  transfers between devices with their start and end apart: 6 -> 5, of which waited for: 6 -> 5; matrix products, arithmetic and copies ran while one was open for 0% -> 0% of each run, Pallas kernels for 0% -> 0%
where the time goes in v1:
time: 850 us; the launch traced here: 849 us
  waiting for transfers between devices  634 us (75%)
  blocking collectives  97 us (11%)
  other arithmetic  61.3 us (7%)
  matrix products  24.9 us (3%)
  local copies, waits for them, and re-layouts  16.2 us (2%)
  between operations  15.4 us (2%)
    psum x1, waiting for transfers between devices, shards(): lax.psum((jnp.dot(whitened.T, whitened, precision=high), jnp.dot(white_ro...  182 us
    psum x1, waiting for transfers between devices, shards(): lax.psum((cross_part, jnp.sum(centred * centred, axis=0)), 'tensor')  174 us
    reduce_scatter x1, waiting for transfers between devices, shards(): lax.psum_scatter(lax.optimization_barrier(partial_value).astype(jnp.float...  131 us
    all_gather x1, waiting for transfers between devices, shards(): lax.all_gather(hidden, 'dp', axis=0, tiled=True)  73.7 us
    reduce_scatter x1, waiting for transfers between devices, shards(): lax.psum_scatter(partial_out, 'tensor', scatter_dimension=0, tiled=True)  73.1 us
    psum x2, blocking collectives, shards(): lax.psum((jnp.sum(output, axis=0), jnp.sum(onehot, axis=0)), 'tensor')  63.4 us
    another operation x6, other arithmetic, shards(): jnp.linalg.cholesky(gram_mat + ridge_term * jnp.eye(NCLS, dtype=jnp.float...  34 us
    all_to_all x1, blocking collectives, shards(): lax.all_to_all(jnp.stack([tokens] * lax.axis_size('tensor')), 'tensor', 0...  33.7 us
  transfers between devices with their start and end apart: 5, of which 5 were waited for; matrix products, arithmetic and copies ran while one was open for 0% of the time, Pallas kernels for 0%

profile of v1, /device:TPU:1, one launch (start us, length us, event | category | flops | bytes accessed | tf_op | source)
XLA Modules:
  0.0 848.9 jit_solution(795846868988800062)
XLA Ops:
  6.5 1.1 stack.2
  7.6 33.7 %all_to_all.5 = bf16[16,64,512]{2,1,0:T(8,128)(2,1)S(1)} all-to-all(bf16[16,64,512]{2,1,0:T(8,128)(2,1)S(1)} %stack.2), channel_id=1, replica_groups=mesh['dp'=16,'tensor'=16] {'tensor'}, dimensions={0} | all-to-all | bytes 2097152 | tf_op jit(solution)/shard_map/all_to_all | solution.py:18
  41.3 8.3 convert_bitcast_fusion
  49.6 10.3 %copy.34 = bf16[1024,3696]{1,0:T(8,128)(2,1)} copy(bf16[1024,3696]{0,1:T(8,128)(2,1)} %convert_bitcast_fusion) | data formatting | bytes 15138816
  60.0 131.1 %reduce-scatter.7.cloned.1.call-done = bf16[64,3696]{1,0:T(8,128)(2,1)} async-done(((bf16[1024,3696]{1,0:T(8,128)(2,1)}), bf16[64,3696]{1,0:T(8,128)(2,1)}) %reduce-scatter.7.cloned.1.call-update) | async-done | bytes 473104 | tf_op jit(solution)/shard_map/reduce_scatter | solution.py:24
  191.0 1.1 convert_element_type.23
  192.1 0.9 fusion.5
  193.1 73.7 %all-gather.2.cloned.1.call-done = bf16[1024,1848]{1,0:T(8,128)(2,1)} async-done(((bf16[64,1848]{1,0:T(8,128)(2,1)}), bf16[1024,1848]{1,0:T(8,128)(2,1)}) %all-gather.2.cloned.1.call-update) | async-done | bytes 3784720 | tf_op jit(solution)/shard_map/all_gather | solution.py:32
  266.9 5.8 fusion.34
  272.8 73.1 %reduce-scatter.5.cloned.1.call-done = f32[64,512]{1,0:T(8,128)} async-done(((f32[1024,512]{1,0:T(8,128)}), f32[64,512]{1,0:T(8,128)}) %reduce-scatter.5.cloned.1.call-update) | async-done | bytes 131088 | tf_op jit(solution)/shard_map/reduce_scatter | solution.py:36
  345.9 0.9 reduce_sum.37
  346.9 31.3 %psum.42 = f32[512]{0:T(512)S(1)} all-reduce(f32[512]{0:T(512)S(1)} %reduce_sum.37), channel_id=1, replica_groups=mesh['dp'=16,'tensor'=16] {'tensor'}, use_global_device_ids=true, to_apply=%region_3.4 | all-reduce | flops 512 | bytes 4096 | tf_op jit(solution)/shard_map/psum | solution.py:39
  378.1 0.9 multiply_reduce_fusion
  379.1 32.1 %all-reduce.1 = (f32[256]{0:T(256)S(1)}, f32[512]{0:T(512)S(1)}) all-reduce(f32[256]{0:T(256)S(1)} %convert_reduce_fusion, f32[512]{0:T(512)S(1)} %multiply_reduce_fusion), channel_id=1, replica_groups=mesh['dp'=16,'tensor'=16] {'tensor'}, use_global_device_ids=true, to_apply=%region_5.6 | all-reduce | flops 768 | bytes 6144 | tf_op jit(solution)/shard_map/psum | solution.py:39
  411.2 2.4 fusion.10
  413.8 173.7 %all-reduce.6.cloned.1.call-done = f32[512,256]{1,0:T(8,128)} async-done(((f32[512,256]{1,0:T(8,128)}), f32[512,256]{1,0:T(8,128)}) %all-reduce.6.cloned.1.call-update) | async-done | bytes 524304 | tf_op jit(solution)/shard_map/psum | solution.py:44
  587.5 2.2 fusion.7
  589.8 3.1 fusion.32
  592.9 182.0 %all-reduce.8.cloned.1.call-done = (f32[256,256]{0,1:T(8,128)}, f32[256,64]{0,1:T(8,128)}) async-done(((f32[256,256]{0,1:T(8,128)}, f32[256,64]{0,1:T(8,128)}), (f32[256,256]{0,1:T(8,128)}, f32[256,64]{0,1:T(8,128)})) %all-reduce.8.cloned.1.call-update) | async-done | bytes 327696 | tf_op jit(solution)/shard_map/psum | solution.py:50
  774.9 1.6 select_reduce_fusion
  777.2 1.0 select_add_fusion
  778.3 1.0 fusion.6
  779.3 11.7 %cholesky.49 = f32[128,128]{1,0:T(8,128)S(1)} custom-call(f32[128,128]{1,0:T(8,128)S(1)} %cholesky.115), custom_call_target="Cholesky" | custom-call | tf_op jit(solution)/shard_map/jit(cholesky)/cholesky | solution.py:58
  791.1 9.8 %custom-call.18 = f32[1,128,128]{1,2,0:T(8,128)S(1)} custom-call(f32[1,128,128]{2,1,0:T(8,128)S(1)} %get-tuple-element.44), custom_call_target="InvertDiagBlocksLowerTriangular" | custom-call | tf_op jit(solution)/shard_map/jit(cholesky)/cholesky | solution.py:58
  801.4 11.7 %cholesky.103 = f32[128,128]{1,0:T(8,128)S(1)} custom-call(f32[128,128]{1,0:T(8,128)S(1)} %convolution_subtract_fusion), custom_call_target="Cholesky" | custom-call | tf_op jit(solution)/shard_map/jit(cholesky)/cholesky | solution.py:58
  813.5 0.7 compare_reduce_fusion
  815.7 4.3 while.1
  815.7 0.6 fusion.46
  816.3 1.4 dynamic-slice.7
  818.4 1.4 dynamic-slice.7
  820.0 19.7 %custom-call.19 = f32[2,128,128]{1,2,0:T(8,128)S(1)} custom-call(f32[2,128,128]{2,1,0:T(8,128)S(1)} %get-tuple-element.12), custom_call_target="InvertDiagBlocksLowerTriangular" | custom-call | tf_op jit(solution)/shard_map/jit(_cho_solve)/triangular_solve | solution.py:59
  841.0 1.3 fusion.4
  (53 shorter events, 3.8 us)
Async XLA Ops:
  6.5 260.3 %copy-start = (bf16[1848,512]{1,0:T(8,128)(2,1)S(1)}, bf16[1848,512]{1,0:T(8,128)(2,1)}, u32[]{:S(2)}) copy-start(bf16[1848,512]{1,0:T(8,128)(2,1)} %param.8) | copy-start | bytes 5677060
  6.5 184.5 %reduce-scatter.7.cloned.1.call-start = ((), (), s32[]{:S(2)}) async-start(), calls=%async_computation.6 | async-start | bytes 8077312 | tf_op jit(solution)/shard_map/reduce_scatter | solution.py:24
  59.9 206.9 %all-gather.2.cloned.1.call-start = ((), (), s32[]{:S(2)}) async-start(), calls=%async_computation.3 | async-start | bytes 4177920 | tf_op jit(solution)/shard_map/all_gather | solution.py:32
  193.1 79.7 %copy-start.3 = (s32[64]{0:T(128)S(1)}, s32[64]{0:T(128)}, u32[]{:S(2)}) copy-start(s32[64]{0:T(128)} %param.9) | copy-start | bytes 772
  193.1 152.9 %reduce-scatter.5.cloned.1.call-start = ((), (), s32[]{:S(2)}) async-start(), calls=%async_computation.4 | async-start | bytes 2228224 | tf_op jit(solution)/shard_map/reduce_scatter | solution.py:36
  272.7 314.9 %all-reduce.6.cloned.1.call-start = ((), (), s32[]{:S(2)}) async-start(), calls=%async_computation.5 | async-start | bytes 1048576 | tf_op jit(solution)/shard_map/psum | solution.py:44
  413.6 361.3 %all-reduce.8.cloned.1.call-start = ((), (), s32[]{:S(2)}) async-start(), calls=%async_computation.7 | async-start | bytes 655360 | tf_op jit(solution)/shard_map/psum | solution.py:50
  592.9 248.1 %copy-start.1 = (f32[64,512]{1,0:T(8,128)S(1)}, f32[64,512]{1,0:T(8,128)}, u32[]{:S(2)}) copy-start(f32[64,512]{1,0:T(8,128)} %reduce-scatter.5.cloned.1.call-done) | copy-start | bytes 393220
  592.9 248.1 %copy-start.4 = (f32[512,256]{1,0:T(8,128)S(1)}, f32[512,256]{1,0:T(8,128)}, u32[]{:S(2)}) copy-start(f32[512,256]{1,0:T(8,128)} %all-reduce.6.cloned.1.call-done) | copy-start | bytes 1572868
  774.9 64.8 %copy-start.2 = (f32[256,64]{0,1:T(8,128)S(1)}, f32[256,64]{0,1:T(8,128)}, u32[]{:S(2)}) copy-start(f32[256,64]{0,1:T(8,128)} %get-tuple-element.40) | copy-start | bytes 196612
Sparse Core Ops, SparseCore 0:
  60.0 130.9 reduce-scatter.6
  194.1 72.7 all-gather.1
  272.8 73.1 reduce-scatter.4
  413.7 173.7 all-reduce.5
  593.0 181.8 all-reduce.7
